TPU v7x, 32 devices: a whole 2x2x4 slice. The times are simulated.
32 devices in a mesh: dp: 8 (over z, x), tensor: 4 (over y, core).
Axes of the slice: x: 2, y: 2, z: 4, core: 2. Of those that a mesh axis runs over, the one named last changes fastest.
Arguments:
- source_rows: bfloat16 [2, 2048, 3072], P(None, ('dp', 'tensor')), may hold values from -6 to 6
- gate_weight: bfloat16 [2, 3072, 9216], P(None, 'dp', 'tensor'), may hold values from -0.15625 to 0.15625
- up_weight: bfloat16 [2, 3072, 9216], P(None, 'dp', 'tensor'), may hold values from -0.15625 to 0.15625
- keep_mask: int32 [2, 2, 48, 144], replicated, may hold values from 0 to 1, as said below
Outputs:
- hidden: bfloat16 [2, 2048, 9216], P(None, 'dp', 'tensor')
Inputs may be any that keep to these rules, and one draw needn't show every extreme that they name: `keep_mask`: within each device's share of a projection (6 x 36 blocks: block rows of one dp index, block columns of one tensor index) at least one and at most 108 blocks are kept, and for each direction and projection some share keeps exactly 108.
All inputs are finite; a program needn't handle non-finite values.
Results may differ from a plain program's by a relative error of at most 0.001.
Values may be sent and summed in bfloat16 or wider, within the bound.
No kernel may reach another device: no remote copies, remote signals or barrier semaphores. Data moves between devices by JAX's collectives and lax.ppermute only.
A program may use at most 192 MiB of HBM per device.

v0:
```python
import jax
import jax.numpy as jnp
from jax import lax
from jax.sharding import PartitionSpec as P

BLOCK = 64


def expand_blocks(block_mask, block_width):
    return jnp.repeat(jnp.repeat(block_mask, block_width, axis=-2), block_width, axis=-1)


def shards(source_rows, gate_weight, up_weight, keep_mask):
    token_slab = lax.all_gather(source_rows, "tensor", axis=1, tiled=True)
    row_blocks = gate_weight.shape[1] // BLOCK
    col_blocks = gate_weight.shape[2] // BLOCK
    dp_index = lax.axis_index("dp")
    tensor_index = lax.axis_index("tensor")
    mask_cols = lax.dynamic_slice_in_dim(keep_mask, tensor_index * col_blocks, col_blocks, 3)
    own_mask = lax.dynamic_slice_in_dim(mask_cols, dp_index * row_blocks, row_blocks, 2)
    stacked = jnp.stack([gate_weight, up_weight], axis=1)
    kept_rows = stacked * expand_blocks(own_mask, BLOCK).astype(jnp.bfloat16)
    weights = lax.all_gather(kept_rows, "dp", axis=2, tiled=True)
    gate_sum = jnp.einsum(
        "mgd,mdf->mgf", token_slab, weights[:, 0], preferred_element_type=jnp.float32
    )
    up_sum = jnp.einsum(
        "mgd,mdf->mgf", token_slab, weights[:, 1], preferred_element_type=jnp.float32
    )
    return (jax.nn.silu(gate_sum) * up_sum).astype(jnp.bfloat16)


def solution(mesh):
    placed = (
        P(None, ("dp", "tensor"), None),
        P(None, "dp", "tensor"),
        P(None, "dp", "tensor"),
        P(),
    )
    return jax.shard_map(
        shards, mesh=mesh, in_specs=placed, out_specs=P(None, "dp", "tensor"), check_vma=False
    )
```

profile of v0, /device:TPU:0, one launch (start us, length us, event | category | flops | bytes accessed | tf_op | source)
XLA Modules:
  0.0 1152.1 jit_solution(3198824043148178128)
XLA Ops:
  6.5 0.0 all-gather.5.cloned.1.call-start
  6.5 0.7 all-gather.5.cloned.1.call-update
  7.3 0.0 all-gather.3.cloned.1.call-start
  7.3 0.9 dynamic-slice_convert_fusion
  8.2 0.1 copy.11
  8.4 0.2 broadcast_in_dim.6
  8.6 0.2 convert_element_type.15
  8.8 0.7 copy.12
  9.5 4.6 copy.9
  14.1 5.8 copy.10
  20.0 5.9 maximum_multiply_fusion
  25.9 0.0 all-gather.3.cloned.1.call-update
  26.0 14.2 %all-gather.5.cloned.1.call-done = bf16[2,256,3072]{2,1,0:T(8,128)(2,1)} async-done(((bf16[2,64,3072]{2,1,0:T(8,128)(2,1)}), bf16[2,256,3072]{2,1,0:T(8,128)(2,1)}) %all-gather.5.cloned.1.call-update) | async-done | bytes 3145744 | tf_op jit(solution)/shard_map/all_gather | solution.py:14
  40.2 1071.8 %all-gather.3.cloned.1.call-done = bf16[2,2,3072,2304]{2,3,0,1:T(8,128)(2,1)} async-done(((bf16[2,2,384,2304]{2,3,0,1:T(8,128)(2,1)}), bf16[2,2,3072,2304]{2,3,0,1:T(8,128)(2,1)}) %all-gather.3.cloned.1.call-update) | async-done | bytes 56623120 | tf_op jit(solution)/shard_map/all_gather | solution.py:23
  1112.0 15.3 %fusion.2 = f32[2,256,2304]{1,2,0:T(8,128)} fusion(bf16[2,256,3072]{2,1,0:T(8,128)(2,1)} %all-gather.5.cloned.1.call-done, bf16[2,2,3072,2304]{2,3,0,1:T(8,128)(2,1)} %all-gather.3.cloned.1.call-done), kind=kOutput, calls=%fused_computation.5 | convolution fusion | flops 7247757312 | bytes 36175872 | tf_op jit(solution)/shard_map/mgd,mdf->mgf/dot_general | solution.py:24
  1127.2 15.6 %fusion.5 = bf16[2,256,2304]{1,2,0:T(8,128)(2,1)S(1)} fusion(bf16[2,256,3072]{2,1,0:T(8,128)(2,1)} %all-gather.5.cloned.1.call-done, bf16[2,2,3072,2304]{2,3,0,1:T(8,128)(2,1)} %all-gather.3.cloned.1.call-done, f32[2,256,2304]{1,2,0:T(8,128)} %fusion.2), kind=kOutput, calls=%fused_computation.8 | convolution fusion | flops 7254835200 | bytes 38535168 | tf_op jit(solution)/shard_map/mgd,mdf->mgf/dot_general | solution.py:27
  1142.9 2.4 copy.13
Async XLA Ops:
  6.5 33.6 %all-gather.5.cloned.1.call-start = ((), (), s32[]{:S(2)}) async-start(), calls=%async_computation.1 | async-start | bytes 3932160 | tf_op jit(solution)/shard_map/all_gather | solution.py:14
  7.3 1104.7 %all-gather.3.cloned.1.call-start = ((), (), s32[]{:S(2)}) async-start(), calls=%async_computation | async-start | bytes 63700992 | tf_op jit(solution)/shard_map/all_gather | solution.py:23
Sparse Core Ops, SparseCore 0:
  8.9 31.2 all-gather.4
  41.7 1070.2 all-gather.2
where the time goes:
time: 1150 us
  waiting for transfers between devices  1090 us (95%)
  matrix products  30.9 us (3%)
  local copies, waits for them, and re-layouts  14.2 us (1%)
  between operations  13.4 us (1%)
    all_gather x1, waiting for transfers between devices, shards(): weights = lax.all_gather(kept_rows, 'dp', axis=2, tiled=True)  1070 us
  transfers between devices with their start and end apart: 2, of which 2 were waited for; matrix products, arithmetic and copies ran while one was open for 2% of the time, Pallas kernels for 0%

commit v1 on v0

--- a/solution.py
+++ b/solution.py
@@ -20,7 +20,16 @@
     own_mask = lax.dynamic_slice_in_dim(mask_cols, dp_index * row_blocks, row_blocks, 2)
     stacked = jnp.stack([gate_weight, up_weight], axis=1)
     kept_rows = stacked * expand_blocks(own_mask, BLOCK).astype(jnp.bfloat16)
-    weights = lax.all_gather(kept_rows, "dp", axis=2, tiled=True)
+    n_parts = lax.axis_size("dp")
+    log = [kept_rows]
+    for pp in tuple(range(1, n_parts)):
+        heard = lax.ppermute(
+            log[pp - 1], axis_name="dp", perm=[(p, (p - 1) % n_parts) for p in range(n_parts)]
+        )
+        log.append(heard)
+    z = jnp.concatenate(log, axis=2)
+    g_now = lax.axis_index("dp")
+    weights = jnp.roll(z, g_now * kept_rows.shape[2], axis=2)
     gate_sum = jnp.einsum(
         "mgd,mdf->mgf", token_slab, weights[:, 0], preferred_element_type=jnp.float32
     )

time: 1150 us -> 1220 us (1.061)
  local copies, waits for them, and re-layouts: 14.2 us -> 113 us
  waiting for transfers between devices: 1090 us -> 1010 us
  starting transfers between devices: 0.04 us -> 37 us
    all_gather x1 -> x0, waiting for transfers between devices: 1070 us -> none  [shards(): weights = lax.all_gather(kept_rows, 'dp', axis=2, tiled=True)]
    ppermute x0 -> x7, waiting for transfers between devices: none -> 1010 us  [shards(): lax.ppermute(log[pp - 1], axis_name='dp', perm=[(p, (p - 1) % n_parts) fo...]
    unnamed x2 -> x50, local copies, waits for them, and re-layouts: 10.5 us -> 103 us
    ppermute x0 -> x7, starting transfers between devices: none -> 37 us  [shards(): lax.ppermute(log[pp - 1], axis_name='dp', perm=[(p, (p - 1) % n_parts) fo...]
    all_gather x1, waiting for transfers between devices: 14.2 us -> 0.01 us  [shards(): token_slab = lax.all_gather(source_rows, 'tensor', axis=1, tiled=True)]
  transfers between devices with their start and end apart: 2 -> 8, of which waited for: 2 -> 7; matrix products, arithmetic and copies ran while one was open for 2% -> 7% of each run, Pallas kernels for 0% -> 0%
where the time goes in v1:
time: 1220 us
  waiting for transfers between devices  1010 us (83%)
  local copies, waits for them, and re-layouts  113 us (9%)
  matrix products  37.5 us (3%)
  starting transfers between devices  37 us (3%)
  between operations  13.5 us (1%)
    ppermute x7, waiting for transfers between devices, shards(): lax.ppermute(log[pp - 1], axis_name='dp', perm=[(p, (p - 1) % n_parts) fo...  1010 us
    unnamed x50, local copies, waits for them, and re-layouts  103 us
    ppermute x7, starting transfers between devices, shards(): lax.ppermute(log[pp - 1], axis_name='dp', perm=[(p, (p - 1) % n_parts) fo...  37 us
  transfers between devices with their start and end apart: 8, of which 7 were waited for; matrix products, arithmetic and copies ran while one was open for 7% of the time, Pallas kernels for 0%

profile of v1, /device:TPU:0, one launch (start us, length us, event | category | flops | bytes accessed | tf_op | source)
XLA Modules:
  0.0 1217.6 jit_solution(6836514860711163510)
XLA Ops:
  8.7 4.6 copy.9
  13.3 5.8 copy.10
  19.1 7.2 constant_dynamic-update-slice_fusion.15
  26.3 5.9 collective-permute-start
  32.2 151.9 %collective-permute-done = bf16[2,2,384,2304]{2,3,0,1:T(8,128)(2,1)S(1)} collective-permute-done((bf16[2,2,384,2304]{2,3,0,1:T(8,128)(2,1)}, bf16[2,2,384,2304]{2,3,0,1:T(8,128)(2,1)S(1)}, u32[]{:S(2)}, u32[]{:S(2)}) %collective-permute-start) | collective-permute-done | bytes 7077920 | tf_op jit(solution)/shard_map/ppermute | solution.py:26
  187.1 5.1 collective-permute-start.1
  192.2 150.8 %collective-permute-done.1 = bf16[2,2,384,2304]{2,3,0,1:T(8,128)(2,1)S(1)} collective-permute-done((bf16[2,2,384,2304]{2,3,0,1:T(8,128)(2,1)S(1)}, bf16[2,2,384,2304]{2,3,0,1:T(8,128)(2,1)S(1)}, u32[]{:S(2)}, u32[]{:S(2)}) %collective-permute-start.1) | collective-permute-done | bytes 7077920 | tf_op jit(solution)/shard_map/ppermute | solution.py:26
  345.8 5.2 collective-permute-start.2
  351.0 149.9 %collective-permute-done.2 = bf16[2,2,384,2304]{2,3,0,1:T(8,128)(2,1)S(1)} collective-permute-done((bf16[2,2,384,2304]{2,3,0,1:T(8,128)(2,1)S(1)}, bf16[2,2,384,2304]{2,3,0,1:T(8,128)(2,1)S(1)}, u32[]{:S(2)}, u32[]{:S(2)}) %collective-permute-start.2) | collective-permute-done | bytes 7077920 | tf_op jit(solution)/shard_map/ppermute | solution.py:26
  503.8 5.2 collective-permute-start.3
  509.0 149.1 %collective-permute-done.3 = bf16[2,2,384,2304]{2,3,0,1:T(8,128)(2,1)S(1)} collective-permute-done((bf16[2,2,384,2304]{2,3,0,1:T(8,128)(2,1)S(1)}, bf16[2,2,384,2304]{2,3,0,1:T(8,128)(2,1)S(1)}, u32[]{:S(2)}, u32[]{:S(2)}) %collective-permute-start.3) | collective-permute-done | bytes 7077920 | tf_op jit(solution)/shard_map/ppermute | solution.py:26
  660.9 5.2 collective-permute-start.4
  666.1 148.2 %collective-permute-done.4 = bf16[2,2,384,2304]{2,3,0,1:T(8,128)(2,1)S(1)} collective-permute-done((bf16[2,2,384,2304]{2,3,0,1:T(8,128)(2,1)S(1)}, bf16[2,2,384,2304]{2,3,0,1:T(8,128)(2,1)S(1)}, u32[]{:S(2)}, u32[]{:S(2)}) %collective-permute-start.4) | collective-permute-done | bytes 7077920 | tf_op jit(solution)/shard_map/ppermute | solution.py:26
  817.1 5.2 collective-permute-start.5
  822.3 147.3 %collective-permute-done.5 = bf16[2,2,384,2304]{2,3,0,1:T(8,128)(2,1)} collective-permute-done((bf16[2,2,384,2304]{2,3,0,1:T(8,128)(2,1)S(1)}, bf16[2,2,384,2304]{2,3,0,1:T(8,128)(2,1)}, u32[]{:S(2)}, u32[]{:S(2)}) %collective-permute-start.5) | collective-permute-done | bytes 7077920 | tf_op jit(solution)/shard_map/ppermute | solution.py:26
  969.6 5.3 collective-permute-start.6
  975.0 7.1 constant_dynamic-update-slice_fusion.14
  982.1 3.8 constant_dynamic-update-slice_fusion.13
  985.9 7.0 constant_dynamic-update-slice_fusion.12
  992.9 7.0 constant_dynamic-update-slice_fusion.11
  1000.0 3.9 constant_dynamic-update-slice_fusion.10
  1003.8 7.0 constant_dynamic-update-slice_fusion.9
  1010.8 110.9 %collective-permute-done.6 = bf16[2,2,384,2304]{2,3,0,1:T(8,128)(2,1)} collective-permute-done((bf16[2,2,384,2304]{2,3,0,1:T(8,128)(2,1)}, bf16[2,2,384,2304]{2,3,0,1:T(8,128)(2,1)}, u32[]{:S(2)}, u32[]{:S(2)}) %collective-permute-start.6) | collective-permute-done | bytes 7077920 | tf_op jit(solution)/shard_map/ppermute | solution.py:26
  1121.7 6.7 constant_dynamic-update-slice_fusion.8
  1128.5 3.8 constant_dynamic-update-slice_fusion.7
  1132.2 3.7 constant_dynamic-update-slice_fusion.6
  1136.0 7.0 constant_dynamic-update-slice_fusion.5
  1150.3 6.8 constant_dynamic-update-slice_fusion.2
  1157.1 6.9 constant_dynamic-update-slice_fusion.1
  1164.0 6.8 constant_dynamic-update-slice_fusion
  1170.8 18.8 %fusion.2 = f32[2,256,2304]{1,2,0:T(8,128)} fusion(bf16[2,256,3072]{2,1,0:T(8,128)(2,1)} %all-gather.2.cloned.1.call-done, bf16[2,2,6144,2304]{2,3,0,1:T(8,128)(2,1)} %constant_dynamic-update-slice_fusion, s32[]{:T(128)S(6)} %select_n.28), kind=kOutput, calls=%fused_computation.5 | convolution fusion | flops 7247757312 | bytes 36175876 | tf_op jit(solution)/shard_map/mgd,mdf->mgf/dot_general | solution.py:33
  1189.5 18.8 %multiply_convert_fusion = bf16[2,256,2304]{1,2,0:T(8,128)(2,1)S(1)} fusion(f32[2,256,2304]{1,2,0:T(8,128)} %fusion.2, bf16[2,256,3072]{2,1,0:T(8,128)(2,1)} %all-gather.2.cloned.1.call-done, bf16[2,2,6144,2304]{2,3,0,1:T(8,128)(2,1)} %constant_dynamic-update-slice_fusion, s32[]{:T(128)S(6)} %add.29, s32[]{:T(128)S(6)} %select_n.28), kind=kOutput, calls=%fused_computation.7 | convolution fusion | flops 7254835200 | bytes 38535176 | tf_op jit(solution)/shard_map/mgd,mdf->mgf/dot_general | solution.py:36
  (51 shorter events, 26.3 us)
Async XLA Ops:
  6.5 1164.2 %all-gather.2.cloned.1.call-start = ((), (), s32[]{:S(2)}) async-start(), calls=%async_computation | async-start | bytes 3932160 | tf_op jit(solution)/shard_map/all_gather | solution.py:14
  26.3 157.9 %collective-permute-start = (bf16[2,2,384,2304]{2,3,0,1:T(8,128)(2,1)}, bf16[2,2,384,2304]{2,3,0,1:T(8,128)(2,1)S(1)}, u32[]{:S(2)}, u32[]{:S(2)}) collective-permute-start(bf16[2,2,384,2304]{2,3,0,1:T(8,128)(2,1)} %get-tuple-element.6), channel_id=1, source_target_pairs={{0,28},{4,0},{8,4},{12,8},{16,12},{20,16},{24,20},{28,24},{1,29},{... | collective-permute-start | bytes 21233672 | tf_op jit(solution)/shard_map/ppermute | solution.py:26
  184.2 2.9 copy-start
  187.1 155.8 %collective-permute-start.1 = (bf16[2,2,384,2304]{2,3,0,1:T(8,128)(2,1)S(1)}, bf16[2,2,384,2304]{2,3,0,1:T(8,128)(2,1)S(1)}, u32[]{:S(2)}, u32[]{:S(2)}) collective-permute-start(bf16[2,2,384,2304]{2,3,0,1:T(8,128)(2,1)S(1)} %collective-permute-done), channel_id=1, source_target_pairs={{0,28},{4,0},{8,4},{12,8},{16,12},{20,16},{24,20},{28,24},{1,29},{... | collective-permute-start | bytes 21233672 | tf_op jit(solution)/shard_map/ppermute | solution.py:26
  342.9 2.9 copy-start.1
  345.8 155.1 %collective-permute-start.2 = (bf16[2,2,384,2304]{2,3,0,1:T(8,128)(2,1)S(1)}, bf16[2,2,384,2304]{2,3,0,1:T(8,128)(2,1)S(1)}, u32[]{:S(2)}, u32[]{:S(2)}) collective-permute-start(bf16[2,2,384,2304]{2,3,0,1:T(8,128)(2,1)S(1)} %collective-permute-done.1), channel_id=1, source_target_pairs={{0,28},{4,0},{8,4},{12,8},{16,12},{20,16},{24,20},{28,24},{1,29},{... | collective-permute-start | bytes 21233672 | tf_op jit(solution)/shard_map/ppermute | solution.py:26
  351.0 631.1 %slice-start.4 = ((s8[7077888]{0:T(1024)(128)(4,1)}), s8[2883584]{0:T(1024)(128)(4,1)S(1)}, s32[]{:S(2)}) async-start(s8[7077888]{0:T(1024)(128)(4,1)} %bitcast.30), calls=%async_computation.5 | async-start | bytes 5767168
  500.9 3.0 copy-start.2
  503.8 154.2 %collective-permute-start.3 = (bf16[2,2,384,2304]{2,3,0,1:T(8,128)(2,1)S(1)}, bf16[2,2,384,2304]{2,3,0,1:T(8,128)(2,1)S(1)}, u32[]{:S(2)}, u32[]{:S(2)}) collective-permute-start(bf16[2,2,384,2304]{2,3,0,1:T(8,128)(2,1)S(1)} %collective-permute-done.2), channel_id=1, source_target_pairs={{0,28},{4,0},{8,4},{12,8},{16,12},{20,16},{24,20},{28,24},{1,29},{... | collective-permute-start | bytes 21233672 | tf_op jit(solution)/shard_map/ppermute | solution.py:26
  658.1 2.8 copy-start.3
  660.9 153.4 %collective-permute-start.4 = (bf16[2,2,384,2304]{2,3,0,1:T(8,128)(2,1)S(1)}, bf16[2,2,384,2304]{2,3,0,1:T(8,128)(2,1)S(1)}, u32[]{:S(2)}, u32[]{:S(2)}) collective-permute-start(bf16[2,2,384,2304]{2,3,0,1:T(8,128)(2,1)S(1)} %collective-permute-done.3), channel_id=1, source_target_pairs={{0,28},{4,0},{8,4},{12,8},{16,12},{20,16},{24,20},{28,24},{1,29},{... | collective-permute-start | bytes 21233672 | tf_op jit(solution)/shard_map/ppermute | solution.py:26
  814.3 2.8 copy-start.4
  817.1 152.5 %collective-permute-start.5 = (bf16[2,2,384,2304]{2,3,0,1:T(8,128)(2,1)S(1)}, bf16[2,2,384,2304]{2,3,0,1:T(8,128)(2,1)}, u32[]{:S(2)}, u32[]{:S(2)}) collective-permute-start(bf16[2,2,384,2304]{2,3,0,1:T(8,128)(2,1)S(1)} %collective-permute-done.4), channel_id=1, source_target_pairs={{0,28},{4,0},{8,4},{12,8},{16,12},{20,16},{24,20},{28,24},{1,29},{... | collective-permute-start | bytes 21233672 | tf_op jit(solution)/shard_map/ppermute | solution.py:26
  969.6 152.1 %collective-permute-start.6 = (bf16[2,2,384,2304]{2,3,0,1:T(8,128)(2,1)}, bf16[2,2,384,2304]{2,3,0,1:T(8,128)(2,1)}, u32[]{:S(2)}, u32[]{:S(2)}) collective-permute-start(bf16[2,2,384,2304]{2,3,0,1:T(8,128)(2,1)} %collective-permute-done.5), channel_id=1, source_target_pairs={{0,28},{4,0},{8,4},{12,8},{16,12},{20,16},{24,20},{28,24},{1,29},{... | collective-permute-start | bytes 21233672 | tf_op jit(solution)/shard_map/ppermute | solution.py:26
  975.0 7.1 slice-start.5
  985.9 14.0 %slice-start.10 = ((s8[7077888]{0:T(1024)(128)(4,1)}), s8[4194304]{0:T(1024)(128)(4,1)S(1)}, s32[]{:S(2)}) async-start(s8[7077888]{0:T(1024)(128)(4,1)} %bitcast.36), calls=%async_computation.11 | async-start | bytes 8388608
  992.9 7.0 slice-start.11
  1003.8 124.6 %slice-start = ((s8[7077888]{0:T(1024)(128)(4,1)}), s8[4194304]{0:T(1024)(128)(4,1)S(1)}, s32[]{:S(2)}) async-start(s8[7077888]{0:T(1024)(128)(4,1)} %bitcast.26), calls=%async_computation.1 | async-start | bytes 8388608
  1010.8 117.7 %slice-start.1 = ((s8[7077888]{0:T(1024)(128)(4,1)}), s8[2883584]{0:T(1024)(128)(4,1)S(1)}, s32[]{:S(2)}) async-start(s8[7077888]{0:T(1024)(128)(4,1)} %bitcast.26), calls=%async_computation.2 | async-start | bytes 5767168
  1010.8 121.4 %slice-start.2 = ((s8[7077888]{0:T(1024)(128)(4,1)}), s8[4194304]{0:T(1024)(128)(4,1)S(1)}, s32[]{:S(2)}) async-start(s8[7077888]{0:T(1024)(128)(4,1)} %bitcast.28), calls=%async_computation.3 | async-start | bytes 8388608
  1128.5 3.8 slice-start.3
  1132.2 10.7 slice-start.6
  1136.0 7.0 slice-start.7
  1136.0 10.7 slice-start.8
  1143.0 3.7 slice-start.9
Sparse Core Ops, SparseCore 0:
  975.1 25.7 all-gather.1
